TPU v7x, 32 devices: a whole 2x2x4 slice. The times are simulated.
32 devices in a mesh: dp: 8 (over z, y), fsdp: 4 (over x, core).
Axes of the slice: x: 2, y: 2, z: 4, core: 2. Of those that a mesh axis runs over, the one named last changes fastest.
Arguments:
- tokens: bfloat16 [2, 8192, 1152], P(None, ('dp', 'fsdp')), may hold values from -6 to 6
- condition: bfloat16 [2, 32, 2, 1152], P(None, ('dp', 'fsdp')), may hold values from -6 to 6
- lengths: int32 [2, 32, 2], P(None, ('dp', 'fsdp')), may hold values from 0 to 256, as said below
- w_mod: bfloat16 [1152, 6912], P('fsdp'), may hold values from -0.1875 to 0.1875
- b_mod: float32 [6912], replicated, may hold values from -1.75 to 1.75
- w_qkv: bfloat16 [1152, 3456], P('fsdp'), may hold values from -0.1875 to 0.1875
- b_qkv: float32 [3456], replicated, may hold values from -1.75 to 1.75
- q_gain: float32 [72], replicated, may hold values from 1 to 1.8
- k_gain: float32 [72], replicated, may hold values from 1 to 1.8
- w_o: bfloat16 [1152, 1152], P('fsdp'), may hold values from -0.75 to 0.75
- b_o: float32 [1152], replicated, may hold values from -1.75 to 1.75
- w_gate: bfloat16 [1152, 3072], P('fsdp'), may hold values from -0.1875 to 0.1875
- w_up: bfloat16 [1152, 3072], P('fsdp'), may hold values from -0.1875 to 0.1875
- w_down: bfloat16 [3072, 1152], P('fsdp'), may hold values from -0.109375 to 0.109375
- d_out: bfloat16 [2, 8192, 1152], P(None, ('dp', 'fsdp')), may hold values from -6 to 6
Outputs:
- block_out: bfloat16 [2, 8192, 1152], P(None, ('dp', 'fsdp'))
- d_tokens: float32 [2, 8192, 1152], P(None, ('dp', 'fsdp'))
- d_condition: float32 [2, 32, 2, 1152], P(None, ('dp', 'fsdp'))
- g_mod: float32 [1152, 6912], P('fsdp')
- g_bmod: float32 [6912], replicated
- g_qkv: float32 [1152, 3456], P('fsdp')
- g_bqkv: float32 [3456], replicated
- g_qgain: float32 [72], replicated
- g_kgain: float32 [72], replicated
- g_o: float32 [1152, 1152], P('fsdp')
- g_bo: float32 [1152], replicated
- g_gate: float32 [1152, 3072], P('fsdp')
- g_up: float32 [1152, 3072], P('fsdp')
- g_down: float32 [3072, 1152], P('fsdp')
Inputs may be any that keep to these rules, and one draw needn't show every extreme that they name: `lengths`: each packed row of 256 tokens holds either one image of 256 patches in slot 0 (slot 1 empty, length 0) or two images of 128 patches; every image has 16 rows of patches; the first row of every micro-batch holds one image.
All inputs are finite; a program needn't handle non-finite values.
Results may differ from a plain program's by a relative error of at most 0.019.
Values may be sent and summed in bfloat16 or wider, within the bound.
No kernel may reach another device: no remote copies, remote signals or barrier semaphores. Data moves between devices by JAX's collectives and lax.ppermute only.
A program may use at most 320 MiB of HBM per device.

v0:
```python
from functools import partial
import jax
import jax.numpy as jnp
from jax import lax
from jax.sharding import PartitionSpec as P

GRID_H = 16
EPSILON = 1e-06
MASKED = -1e30


def silu_grad(values):
    sigmoid = jax.nn.sigmoid(values)
    return sigmoid * (1.0 + values * (1.0 - sigmoid))


def pack_layout(lengths_row, row_count):
    slot_count = lengths_row.shape[0]
    slot_ends = jnp.cumsum(lengths_row)
    slot_starts = slot_ends - lengths_row
    tok_index = jnp.arange(row_count, dtype=jnp.int32)
    segment = jnp.sum(
        (tok_index[:, None] >= slot_ends[None, : slot_count - 1]).astype(jnp.int32), axis=1
    )
    slot_ids = jnp.arange(slot_count, dtype=jnp.int32)
    member = segment[:, None] == slot_ids[None, :]
    offset = jnp.sum(jnp.where(member, slot_starts[None, :], 0), axis=1)
    widths = jnp.maximum(lengths_row // GRID_H, 1)
    tok_width = jnp.sum(jnp.where(member, widths[None, :], 0), axis=1)
    position = tok_index - offset
    return (segment, member.astype(jnp.float32), position // tok_width, position % tok_width)


def rope_angles(grid_row, grid_col, head_dim):
    quarter = head_dim // 4
    frequency = 10000.0 ** (-jnp.arange(quarter, dtype=jnp.float32) / quarter)
    angle_table = jnp.concatenate(
        [
            grid_row.astype(jnp.float32)[:, None] * frequency[None, :],
            grid_col.astype(jnp.float32)[:, None] * frequency[None, :],
        ],
        axis=1,
    )
    return (jnp.cos(angle_table)[:, None, :], jnp.sin(angle_table)[:, None, :])


def norm_mod(field, scale_part, shift_part):
    inverse = lax.rsqrt(jnp.mean(field * field, axis=-1, keepdims=True) + EPSILON)
    return field * inverse * (1.0 + scale_part) + shift_part


def rotate(vector, cosine, sine_table):
    half_dim = vector.shape[-1] // 2
    first = vector[..., :half_dim]
    second = vector[..., half_dim:]
    return jnp.concatenate(
        [first * cosine - second * sine_table, second * cosine + first * sine_table], axis=-1
    )


def head_prep(cosine, sine_table, raw_head, gain_vec):
    inverse = lax.rsqrt(jnp.mean(raw_head * raw_head, axis=-1, keepdims=True) + EPSILON)
    return rotate(raw_head * inverse * gain_vec, cosine, sine_table)


def score_block(q_rot, k_rot, same_slot, score_scale):
    raw_score = jnp.einsum("qhd,khd->hqk", q_rot, k_rot, preferred_element_type=jnp.float32)
    return jnp.where(same_slot[None, :, :], raw_score * score_scale, MASKED)


def forward(row_tokens, row_cond, row_lengths, matrices, minor_params):
    w_mod, w_qkv, w_o, w_gate, w_up, w_down = matrices
    b_mod, b_qkv, q_gain, k_gain, b_o = minor_params
    row_count, model_width = row_tokens.shape
    head_dim = q_gain.shape[0]
    head_count = model_width // head_dim
    segment, member, grid_row, grid_col = pack_layout(row_lengths, row_count)
    cosine, sine_table = rope_angles(grid_row, grid_col, head_dim)
    cond_float = row_cond.astype(jnp.float32)
    silu_cond = jax.nn.silu(cond_float).astype(jnp.bfloat16)
    mod_slots = jnp.dot(silu_cond, w_mod, preferred_element_type=jnp.float32) + b_mod
    mod_tokens = jnp.dot(member, mod_slots, precision=lax.Precision.HIGHEST)
    mod_parts = [
        mod_tokens[:, slot_part * model_width : (slot_part + 1) * model_width]
        for slot_part in range(6)
    ]
    tok_float = row_tokens.astype(jnp.float32)
    norm_one = norm_mod(tok_float, mod_parts[1], mod_parts[0]).astype(jnp.bfloat16)
    qkv_all = jnp.dot(norm_one, w_qkv, preferred_element_type=jnp.float32) + b_qkv
    q_raw = qkv_all[:, :model_width].reshape(row_count, head_count, head_dim)
    k_raw = qkv_all[:, model_width : 2 * model_width].reshape(row_count, head_count, head_dim)
    v_low = (
        qkv_all[:, 2 * model_width :].reshape(row_count, head_count, head_dim).astype(jnp.bfloat16)
    )
    q_rot = head_prep(cosine, sine_table, q_raw, q_gain).astype(jnp.bfloat16)
    k_rot = head_prep(cosine, sine_table, k_raw, k_gain).astype(jnp.bfloat16)
    same_slot = segment[:, None] == segment[None, :]
    score_scale = head_dim ** (-0.5)
    score = score_block(q_rot, k_rot, same_slot, score_scale)
    top_score = jnp.max(score, axis=-1, keepdims=True)
    log_total = top_score + jnp.log(jnp.sum(jnp.exp(score - top_score), axis=-1, keepdims=True))
    attn_prob = jnp.exp(score - log_total)
    attn_out = jnp.einsum(
        "hqk,khd->qhd", attn_prob.astype(jnp.bfloat16), v_low, preferred_element_type=jnp.float32
    )
    attn_out = attn_out.astype(jnp.bfloat16).reshape(row_count, model_width)
    branch = jnp.dot(attn_out, w_o, preferred_element_type=jnp.float32) + b_o
    res_one = tok_float + mod_parts[2] * branch
    norm_two = norm_mod(res_one, mod_parts[4], mod_parts[3]).astype(jnp.bfloat16)
    gate_pre = jnp.dot(norm_two, w_gate, preferred_element_type=jnp.float32)
    up_pre = jnp.dot(norm_two, w_up, preferred_element_type=jnp.float32)
    hidden = (jax.nn.silu(gate_pre) * up_pre).astype(jnp.bfloat16)
    mlp_out = jnp.dot(hidden, w_down, preferred_element_type=jnp.float32)
    block_row = res_one + mod_parts[5] * mlp_out
    stored = {
        "member": member,
        "cosine": cosine,
        "sine_table": sine_table,
        "cond_float": cond_float,
        "silu_cond": silu_cond,
        "mod_parts": mod_parts,
        "tok_float": tok_float,
        "norm_one": norm_one,
        "q_raw": q_raw,
        "k_raw": k_raw,
        "q_rot": q_rot,
        "k_rot": k_rot,
        "v_low": v_low,
        "same_slot": same_slot,
        "log_total": log_total,
        "attn_out": attn_out,
        "branch": branch,
        "res_one": res_one,
        "norm_two": norm_two,
        "gate_pre": gate_pre,
        "up_pre": up_pre,
        "hidden": hidden,
        "mlp_out": mlp_out,
    }
    return (block_row, stored)


def backward(stored, row_grad, matrices, minor_params):
    w_mod, w_qkv, w_o, w_gate, w_up, w_down = matrices
    b_mod, b_qkv, q_gain, k_gain, b_o = minor_params
    row_count, model_width = row_grad.shape
    head_dim = q_gain.shape[0]
    head_count = model_width // head_dim
    score_scale = head_dim ** (-0.5)
    mod_parts = stored["mod_parts"]
    d_mlp = (row_grad * mod_parts[5]).astype(jnp.bfloat16)
    d_gate2 = row_grad * stored["mlp_out"]
    g_down = jnp.dot(stored["hidden"].T, d_mlp, preferred_element_type=jnp.float32)
    d_hidden = jnp.dot(d_mlp, w_down.T, preferred_element_type=jnp.float32)
    gate_pre = stored["gate_pre"]
    d_gate = (d_hidden * stored["up_pre"] * silu_grad(gate_pre)).astype(jnp.bfloat16)
    d_upper = (d_hidden * jax.nn.silu(gate_pre)).astype(jnp.bfloat16)
    g_gate = jnp.dot(stored["norm_two"].T, d_gate, preferred_element_type=jnp.float32)
    g_up = jnp.dot(stored["norm_two"].T, d_upper, preferred_element_type=jnp.float32)
    d_norm_two = jnp.dot(d_gate, w_gate.T, preferred_element_type=jnp.float32) + jnp.dot(
        d_upper, w_up.T, preferred_element_type=jnp.float32
    )
    unused_two, back_two = jax.vjp(norm_mod, stored["res_one"], mod_parts[4], mod_parts[3])
    d_res_norm, d_scale2, d_shift2 = back_two(d_norm_two)
    d_res_one = row_grad + d_res_norm
    d_branch = d_res_one * mod_parts[2]
    d_gate1 = d_res_one * stored["branch"]
    g_bo = jnp.sum(d_branch, axis=0)
    d_proj = d_branch.astype(jnp.bfloat16)
    g_o = jnp.dot(stored["attn_out"].T, d_proj, preferred_element_type=jnp.float32)
    d_attn = (
        jnp.dot(d_proj, w_o.T, preferred_element_type=jnp.float32)
        .astype(jnp.bfloat16)
        .reshape(row_count, head_count, head_dim)
    )
    q_rot = stored["q_rot"]
    k_rot = stored["k_rot"]
    v_low = stored["v_low"]
    score = score_block(q_rot, k_rot, stored["same_slot"], score_scale)
    attn_prob = jnp.exp(score - stored["log_total"])
    d_prob = jnp.einsum("qhd,khd->hqk", d_attn, v_low, preferred_element_type=jnp.float32)
    d_value = jnp.einsum(
        "hqk,qhd->khd", attn_prob.astype(jnp.bfloat16), d_attn, preferred_element_type=jnp.float32
    )
    row_dot = jnp.sum(attn_prob * d_prob, axis=-1, keepdims=True)
    d_score = (attn_prob * (d_prob - row_dot) * score_scale).astype(jnp.bfloat16)
    d_q_rot = jnp.einsum("hqk,khd->qhd", d_score, k_rot, preferred_element_type=jnp.float32)
    d_k_rot = jnp.einsum("hqk,qhd->khd", d_score, q_rot, preferred_element_type=jnp.float32)
    prep_fn = partial(head_prep, stored["cosine"], stored["sine_table"])
    unused_q, back_query = jax.vjp(prep_fn, stored["q_raw"], q_gain)
    d_query, g_qgain = back_query(d_q_rot)
    unused_k, back_key = jax.vjp(prep_fn, stored["k_raw"], k_gain)
    d_key, g_kgain = back_key(d_k_rot)
    d_qkv = jnp.concatenate(
        [
            d_query.reshape(row_count, model_width),
            d_key.reshape(row_count, model_width),
            d_value.reshape(row_count, model_width),
        ],
        axis=1,
    )
    g_bqkv = jnp.sum(d_qkv, axis=0)
    d_qkv_low = d_qkv.astype(jnp.bfloat16)
    g_qkv = jnp.dot(stored["norm_one"].T, d_qkv_low, preferred_element_type=jnp.float32)
    d_norm_one = jnp.dot(d_qkv_low, w_qkv.T, preferred_element_type=jnp.float32)
    unused_one, back_one = jax.vjp(norm_mod, stored["tok_float"], mod_parts[1], mod_parts[0])
    d_tok_norm, d_scale1, d_shift1 = back_one(d_norm_one)
    d_tokens = d_res_one + d_tok_norm
    d_mod_tokens = jnp.concatenate(
        [d_shift1, d_scale1, d_gate1, d_shift2, d_scale2, d_gate2], axis=1
    )
    d_mod = jnp.dot(stored["member"].T, d_mod_tokens, precision=lax.Precision.HIGHEST)
    g_bmod = jnp.sum(d_mod, axis=0)
    d_mod_low = d_mod.astype(jnp.bfloat16)
    g_mod = jnp.dot(stored["silu_cond"].T, d_mod_low, preferred_element_type=jnp.float32)
    d_condition = jnp.dot(d_mod_low, w_mod.T, preferred_element_type=jnp.float32) * silu_grad(
        stored["cond_float"]
    )
    return (
        d_tokens,
        d_condition,
        (g_mod, g_qkv, g_o, g_gate, g_up, g_down),
        (g_bmod, g_bqkv, g_qgain, g_kgain, g_bo),
    )


def sum_data(grad_parts):
    return (
        lax.psum(grad_parts[0].astype(jnp.bfloat16), "dp").astype(jnp.float32),
        lax.psum(grad_parts[1].astype(jnp.bfloat16), "dp").astype(jnp.float32),
        lax.psum(grad_parts[2].astype(jnp.bfloat16), "dp").astype(jnp.float32),
        lax.psum(grad_parts[3].astype(jnp.bfloat16), "dp").astype(jnp.float32),
        lax.psum(grad_parts[4].astype(jnp.bfloat16), "dp").astype(jnp.float32),
        lax.psum(grad_parts[5].astype(jnp.bfloat16), "dp").astype(jnp.float32),
    )


def add_parts(first_parts, second_parts):
    return tuple(
        (left_part + right_part for left_part, right_part in zip(first_parts, second_parts))
    )


def shards(
    tokens,
    condition,
    lengths,
    w_mod,
    b_mod,
    w_qkv,
    b_qkv,
    q_gain,
    k_gain,
    w_o,
    b_o,
    w_gate,
    w_up,
    w_down,
    d_out,
):
    minor_params = (b_mod, b_qkv, q_gain, k_gain, b_o)
    micro_count = tokens.shape[0]
    out_rows = []
    grad_rows = []
    cond_rows = []
    shard_total = None
    minor_total = None
    for micro in range(micro_count):
        matrices = (
            lax.all_gather(w_mod, "fsdp", axis=0, tiled=True),
            lax.all_gather(w_qkv, "fsdp", axis=0, tiled=True),
            lax.all_gather(w_o, "fsdp", axis=0, tiled=True),
            lax.all_gather(w_gate, "fsdp", axis=0, tiled=True),
            lax.all_gather(w_up, "fsdp", axis=0, tiled=True),
            lax.all_gather(w_down, "fsdp", axis=0, tiled=True),
        )
        block_row, stored = forward(
            tokens[micro], condition[micro, 0], lengths[micro, 0], matrices, minor_params
        )
        out_rows.append(block_row.astype(jnp.bfloat16))
        back_matrices = (
            lax.all_gather(w_mod, "fsdp", axis=0, tiled=True),
            lax.all_gather(w_qkv, "fsdp", axis=0, tiled=True),
            lax.all_gather(w_o, "fsdp", axis=0, tiled=True),
            lax.all_gather(w_gate, "fsdp", axis=0, tiled=True),
            lax.all_gather(w_up, "fsdp", axis=0, tiled=True),
            lax.all_gather(w_down, "fsdp", axis=0, tiled=True),
        )
        d_row, d_cond_row, full_grads, minor_grads = backward(
            stored, d_out[micro].astype(jnp.float32), back_matrices, minor_params
        )
        grad_rows.append(d_row)
        cond_rows.append(d_cond_row[None, :, :])
        shard_grads = (
            lax.psum_scatter(
                full_grads[0].astype(jnp.bfloat16), "fsdp", scatter_dimension=0, tiled=True
            ).astype(jnp.float32),
            lax.psum_scatter(
                full_grads[1].astype(jnp.bfloat16), "fsdp", scatter_dimension=0, tiled=True
            ).astype(jnp.float32),
            lax.psum_scatter(
                full_grads[2].astype(jnp.bfloat16), "fsdp", scatter_dimension=0, tiled=True
            ).astype(jnp.float32),
            lax.psum_scatter(
                full_grads[3].astype(jnp.bfloat16), "fsdp", scatter_dimension=0, tiled=True
            ).astype(jnp.float32),
            lax.psum_scatter(
                full_grads[4].astype(jnp.bfloat16), "fsdp", scatter_dimension=0, tiled=True
            ).astype(jnp.float32),
            lax.psum_scatter(
                full_grads[5].astype(jnp.bfloat16), "fsdp", scatter_dimension=0, tiled=True
            ).astype(jnp.float32),
        )
        shard_grads = sum_data(shard_grads)
        shard_total = shard_grads if shard_total is None else add_parts(shard_total, shard_grads)
        minor_total = minor_grads if minor_total is None else add_parts(minor_total, minor_grads)
    minor_sums = lax.psum(
        (minor_total[0], minor_total[1], minor_total[2], minor_total[3], minor_total[4]),
        ("dp", "fsdp"),
    )
    block_out = jnp.stack(out_rows, axis=0)
    d_tokens = jnp.stack(grad_rows, axis=0)
    d_condition = jnp.stack(cond_rows, axis=0)
    return (
        block_out,
        d_tokens,
        d_condition,
        shard_total[0],
        minor_sums[0],
        shard_total[1],
        minor_sums[1],
        minor_sums[2],
        minor_sums[3],
        shard_total[2],
        minor_sums[4],
        shard_total[3],
        shard_total[4],
        shard_total[5],
    )


def solution(mesh):
    placed = (
        P(None, ("dp", "fsdp"), None),
        P(None, ("dp", "fsdp"), None, None),
        P(None, ("dp", "fsdp"), None),
        P("fsdp", None),
        P(),
        P("fsdp", None),
        P(),
        P(),
        P(),
        P("fsdp", None),
        P(),
        P("fsdp", None),
        P("fsdp", None),
        P("fsdp", None),
        P(None, ("dp", "fsdp"), None),
    )
    return jax.shard_map(
        shards,
        mesh=mesh,
        in_specs=placed,
        out_specs=(
            P(None, ("dp", "fsdp"), None),
            P(None, ("dp", "fsdp"), None),
            P(None, ("dp", "fsdp"), None, None),
            P("fsdp", None),
            P(),
            P("fsdp", None),
            P(),
            P(),
            P(),
            P("fsdp", None),
            P(),
            P("fsdp", None),
            P("fsdp", None),
            P("fsdp", None),
        ),
        check_vma=False,
    )
```

profile of v0, /device:TPU:0, one launch (start us, length us, event | category | flops | bytes accessed | tf_op | source)
XLA Modules:
  0.0 2080.1 jit_solution(17581181648474980541)
XLA Ops:
  16.1 97.3 %all-gather.7.cloned.1.call-done = bf16[1152,6912]{1,0:T(8,128)(2,1)} async-done(((bf16[288,6912]{1,0:T(8,128)(2,1)}), bf16[1152,6912]{1,0:T(8,128)(2,1)}) %all-gather.7.cloned.1.call-update) | async-done | bytes 15925264 | tf_op jit(solution)/shard_map/all_gather | solution.py:270
  113.4 7.7 convolution_add_fusion.1
  121.1 3.0 fusion.117
  124.1 3.6 copy-done
  128.0 42.8 %all-gather.9.cloned.1.call-done = bf16[1152,3456]{1,0:T(8,128)(2,1)} async-done(((bf16[288,3456]{1,0:T(8,128)(2,1)}), bf16[1152,3456]{1,0:T(8,128)(2,1)}) %all-gather.9.cloned.1.call-update) | async-done | bytes 7962640 | tf_op jit(solution)/shard_map/all_gather | solution.py:271
  170.8 5.8 convolution_add_fusion.3
  187.9 10.2 all-gather.11.cloned.1.call-done
  198.1 4.6 multiply_reduce_fusion.15
  203.8 2.8 fusion.69
  206.6 43.7 %all-gather.13.cloned.1.call-done = bf16[1152,3072]{1,0:T(8,128)(2,1)} async-done(((bf16[288,3072]{1,0:T(8,128)(2,1)}), bf16[1152,3072]{1,0:T(8,128)(2,1)}) %all-gather.13.cloned.1.call-update) | async-done | bytes 7077904 | tf_op jit(solution)/shard_map/all_gather | solution.py:273
  250.4 7.1 fusion.190
  257.5 45.2 %all-gather.17.cloned.1.call-done = bf16[3072,1152]{1,0:T(8,128)(2,1)} async-done(((bf16[768,1152]{1,0:T(8,128)(2,1)}), bf16[3072,1152]{1,0:T(8,128)(2,1)}) %all-gather.17.cloned.1.call-update) | async-done | bytes 7077904 | tf_op jit(solution)/shard_map/all_gather | solution.py:275
  302.7 7.5 fusion.184
  310.1 44.8 %all-gather.15.cloned.1.call-done = bf16[1152,3072]{1,0:T(8,128)(2,1)} async-done(((bf16[288,3072]{1,0:T(8,128)(2,1)}), bf16[1152,3072]{1,0:T(8,128)(2,1)}) %all-gather.15.cloned.1.call-update) | async-done | bytes 7077904 | tf_op jit(solution)/shard_map/all_gather | solution.py:274
  354.9 8.0 multiply_convert_fusion.7
  363.0 7.0 fusion.195
  370.0 4.1 multiply_reduce_fusion.11
  382.2 3.0 convolution_convert_fusion.13
  386.3 3.5 fusion.95
  389.8 2.7 fusion.196
  392.6 9.9 fusion.44
  402.4 10.1 fusion.47
  418.2 8.1 convolution_add_fusion
  426.3 3.0 fusion.115
  429.4 10.9 fusion.78
  440.3 3.3 fusion.55
  443.7 6.5 convolution_add_fusion.2
  467.2 4.0 fusion.193
  471.2 4.0 fusion.192
  475.2 10.0 multiply_convert_fusion.2
  485.2 6.4 fusion.197
  491.7 6.2 multiply_reduce_fusion.8
  510.8 6.6 convolution_convert_fusion.7
  517.8 6.9 convolution_convert_fusion.9
  524.8 7.0 convolution_convert_fusion.5
  531.9 7.1 convolution_convert_fusion.4
  539.1 6.5 convolution_convert_fusion.6
  545.7 6.6 convolution_convert_fusion.8
  552.4 9.3 convolution_convert_fusion.3
  561.9 4.0 convolution_convert_fusion.12
  568.1 4.3 fusion.198
  572.4 9.7 fusion.38
  582.1 9.9 fusion.41
  601.4 5.9 convolution_convert_fusion.2
  607.9 6.0 fusion.188
  614.5 8.6 convolution_convert_fusion.1
  625.7 9.1 fusion.80
  634.8 2.9 fusion.52
  642.2 3.0 fusion.189
  645.8 7.9 convolution_convert_fusion
  653.8 25.2 %reduce-scatter.25.cloned.1.call-done = bf16[288,3072]{1,0:T(8,128)(2,1)} async-done(((bf16[1152,3072]{1,0:T(8,128)(2,1)}), bf16[288,3072]{1,0:T(8,128)(2,1)}) %reduce-scatter.25.cloned.1.call-update) | async-done | bytes 1769488 | tf_op jit(solution)/shard_map/reduce_scatter | solution.py:304
  679.0 66.8 %reduce-scatter.33.cloned.1.call-done = bf16[768,1152]{1,0:T(8,128)(2,1)} async-done(((bf16[3072,1152]{1,0:T(8,128)(2,1)}), bf16[768,1152]{1,0:T(8,128)(2,1)}) %reduce-scatter.33.cloned.1.call-update) | async-done | bytes 1769488 | tf_op jit(solution)/shard_map/reduce_scatter | solution.py:310
  745.8 66.6 %reduce-scatter.35.cloned.1.call-done = bf16[768,1152]{1,0:T(8,128)(2,1)} async-done(((bf16[3072,1152]{1,0:T(8,128)(2,1)}), bf16[768,1152]{1,0:T(8,128)(2,1)}) %reduce-scatter.35.cloned.1.call-update) | async-done | bytes 1769488 | tf_op jit(solution)/shard_map/reduce_scatter | solution.py:310
  812.4 66.8 %reduce-scatter.31.cloned.1.call-done = bf16[288,3072]{1,0:T(8,128)(2,1)} async-done(((bf16[1152,3072]{1,0:T(8,128)(2,1)}), bf16[288,3072]{1,0:T(8,128)(2,1)}) %reduce-scatter.31.cloned.1.call-update) | async-done | bytes 1769488 | tf_op jit(solution)/shard_map/reduce_scatter | solution.py:307
  879.2 66.6 %reduce-scatter.27.cloned.1.call-done = bf16[288,3072]{1,0:T(8,128)(2,1)} async-done(((bf16[1152,3072]{1,0:T(8,128)(2,1)}), bf16[288,3072]{1,0:T(8,128)(2,1)}) %reduce-scatter.27.cloned.1.call-update) | async-done | bytes 1769488 | tf_op jit(solution)/shard_map/reduce_scatter | solution.py:304
  945.8 71.4 %reduce-scatter.17.cloned.1.call-done = bf16[288,3456]{1,0:T(8,128)(2,1)} async-done(((bf16[1152,3456]{1,0:T(8,128)(2,1)}), bf16[288,3456]{1,0:T(8,128)(2,1)}) %reduce-scatter.17.cloned.1.call-update) | async-done | bytes 1990672 | tf_op jit(solution)/shard_map/reduce_scatter | solution.py:298
  1017.2 71.9 %reduce-scatter.19.cloned.1.call-done = bf16[288,3456]{1,0:T(8,128)(2,1)} async-done(((bf16[1152,3456]{1,0:T(8,128)(2,1)}), bf16[288,3456]{1,0:T(8,128)(2,1)}) %reduce-scatter.19.cloned.1.call-update) | async-done | bytes 1990672 | tf_op jit(solution)/shard_map/reduce_scatter | solution.py:298
  1089.1 122.6 %reduce-scatter.13.cloned.1.call-done = bf16[288,6912]{1,0:T(8,128)(2,1)} async-done(((bf16[1152,6912]{1,0:T(8,128)(2,1)}), bf16[288,6912]{1,0:T(8,128)(2,1)}) %reduce-scatter.13.cloned.1.call-update) | async-done | bytes 3981328 | tf_op jit(solution)/shard_map/reduce_scatter | solution.py:295
  1211.6 122.6 %reduce-scatter.15.cloned.1.call-done = bf16[288,6912]{1,0:T(8,128)(2,1)} async-done(((bf16[1152,6912]{1,0:T(8,128)(2,1)}), bf16[288,6912]{1,0:T(8,128)(2,1)}) %reduce-scatter.15.cloned.1.call-update) | async-done | bytes 3981328 | tf_op jit(solution)/shard_map/reduce_scatter | solution.py:295
  1339.6 44.6 %all-reduce.8 = (f32[6912]{0:T(1024)}, f32[3456]{0:T(1024)}, f32[72]{0:T(128)}, f32[72]{0:T(128)}, f32[1152]{0:T(1024)}) all-reduce(f32[6912]{0:T(1024)S(1)} %add.442, f32[3456]{0:T(1024)S(1)} %add.444, f32[72]{0:T(128)S(1)} %copy-done.143, f32[72]{0:T(128)S(1)} %add.446, ...), channel_id=1, replica_groups=mesh['dp'=8,'fsdp'=4] {'dp','fsdp'}, use_global_device_ids=true, to_apply=%region_34.35 | all-reduce | flops 11664 | bytes 93312 | tf_op jit(solution)/shard_map/psum | solution.py:317
  1384.2 9.8 fusion.28
  1394.0 10.2 fusion.29
  1407.6 643.9 %all-reduce.12.cloned.1.call-done = (bf16[288,6912]{1,0:T(8,128)(2,1)}, bf16[288,6912]{1,0:T(8,128)(2,1)}, bf16[288,3456]{1,0:T(8,128)(2,1)}, bf16[288,3456]{1,0...) async-done(((bf16[288,6912]{1,0:T(8,128)(2,1)}, ...) | async-done | bytes 23887888 | tf_op jit(solution)/shard_map/psum | solution.py:229
  2051.5 7.5 convert_add_fusion
  (467 shorter events, 109.4 us)
Async XLA Ops:
  7.2 106.2 %all-gather.7.cloned.1.call-start = ((), (), s32[]{:S(2)}) async-start(), calls=%async_computation.12 | async-start | bytes 19906560 | tf_op jit(solution)/shard_map/all_gather | solution.py:270
  7.9 162.9 %all-gather.9.cloned.1.call-start = ((), (), s32[]{:S(2)}) async-start(), calls=%async_computation.13 | async-start | bytes 9953280 | tf_op jit(solution)/shard_map/all_gather | solution.py:271
  8.7 189.5 %all-gather.11.cloned.1.call-start = ((), (), s32[]{:S(2)}) async-start(), calls=%async_computation.14 | async-start | bytes 3317760 | tf_op jit(solution)/shard_map/all_gather | solution.py:272
  9.4 241.0 %all-gather.13.cloned.1.call-start = ((), (), s32[]{:S(2)}) async-start(), calls=%async_computation.15 | async-start | bytes 8847360 | tf_op jit(solution)/shard_map/all_gather | solution.py:273
  10.0 292.7 %all-gather.17.cloned.1.call-start = ((), (), s32[]{:S(2)}) async-start(), calls=%async_computation.17 | async-start | bytes 8847360 | tf_op jit(solution)/shard_map/all_gather | solution.py:275
  10.6 102.8 %copy-start.102 = (bf16[2,1,2,1152]{3,2,1,0:T(2,128)(2,1)S(1)}, bf16[2,1,2,1152]{3,2,1,0:T(2,128)(2,1)}, u32[]{:S(2)}) copy-start(bf16[2,1,2,1152]{3,2,1,0:T(2,128)(2,1)} %param.16) | copy-start | bytes 27652
  10.6 102.8 %copy-start.105 = (f32[6912]{0:T(1024)S(1)}, f32[6912]{0:T(1024)}, u32[]{:S(2)}) copy-start(f32[6912]{0:T(1024)} %param.19) | copy-start | bytes 82948
  10.6 344.3 %all-gather.15.cloned.1.call-start = ((), (), s32[]{:S(2)}) async-start(), calls=%async_computation.16 | async-start | bytes 8847360 | tf_op jit(solution)/shard_map/all_gather | solution.py:274
  11.2 642.5 %reduce-scatter.21.cloned.1.call-start = ((), (), s32[]{:S(2)}) async-start(), calls=%async_computation.22 | async-start | bytes 3317760 | tf_op jit(solution)/shard_map/reduce_scatter | solution.py:301
  11.7 109.3 %copy-start.112 = (s32[256]{0:T(256)}, s32[256]{0:T(256)S(1)}, u32[]{:S(2)}) copy-start(s32[256]{0:T(256)S(1)} %compare_convert_fusion.1) | copy-start | bytes 3076
  14.6 109.5 %copy-start.133 = (f32[256]{0:T(256)}, f32[256]{0:T(256)S(1)}, u32[]{:S(2)}) copy-start(f32[256]{0:T(256)S(1)} %fusion.126) | copy-start | bytes 3076
  127.7 43.1 %copy-start.145 = (f32[3456]{0:T(1024)S(1)}, f32[3456]{0:T(1024)}, u32[]{:S(2)}) copy-start(f32[3456]{0:T(1024)} %param.21) | copy-start | bytes 41476
  128.0 48.6 %copy-start.47 = (bf16[256,1152]{1,0:T(8,128)(2,1)}, bf16[256,1152]{1,0:T(8,128)(2,1)S(1)}, u32[]{:S(2)}) copy-start(bf16[256,1152]{1,0:T(8,128)(2,1)S(1)} %fusion.54) | copy-start | bytes 1769476
  202.7 173.8 %copy-start.2 = (f32[256,1152]{1,0:T(8,128)}, f32[256,1152]{1,0:T(8,128)S(1)}, u32[]{:S(2)}) copy-start(f32[256,1152]{1,0:T(8,128)S(1)} %get-tuple-element.55) | copy-start | bytes 3538948
  363.0 7.0 copy-start.65
  363.0 7.0 copy-start.66
  363.0 11.2 copy-start.43
  363.0 7.0 copy-start.144
  363.0 11.2 slice-start.4
  370.0 4.2 slice-start.5
  370.0 6.5 slice-start
  389.8 39.5 %copy-start.28 = (f32[16,72,256]{2,1,0:T(8,128)}, f32[16,72,256]{2,1,0:T(8,128)S(1)}, u32[]{:S(2)}) copy-start(f32[16,72,256]{2,1,0:T(8,128)S(1)} %fusion.95) | copy-start | bytes 3538948
  416.0 13.3 copy-start.11
  418.2 11.2 copy-start.13
  418.2 8.1 copy-start.110
  429.3 11.0 copy-start.1
  429.3 10.9 copy-start.132
  429.4 11.0 copy-start.134
  443.7 6.5 copy-start.45
  451.4 202.3 %reduce-scatter.23.cloned.1.call-start = ((), (), s32[]{:S(2)}) async-start(), calls=%async_computation.23 | async-start | bytes 3317760 | tf_op jit(solution)/shard_map/reduce_scatter | solution.py:301
  457.8 5.6 slice-start.2
  458.8 4.6 slice-start.3
  462.3 4.9 slice-start.10
  466.9 38.4 %copy-start.127 = (f32[256]{0:T(256)}, f32[256]{0:T(256)S(1)}, u32[]{:S(2)}) copy-start(f32[256]{0:T(256)S(1)} %fusion.129) | copy-start | bytes 3076
  466.9 4.3 slice-start.8
  485.2 6.4 copy-start.67
  485.2 17.7 copy-start.44
  485.2 17.7 slice-start.6
  491.7 6.2 copy-start.21
  491.7 6.2 copy-start.35
  491.7 11.2 slice-start.7
  497.9 7.4 copy-start.23
  510.7 143.1 %reduce-scatter.29.cloned.1.call-start = ((), (), s32[]{:S(2)}) async-start(), calls=%async_computation.26 | async-start | bytes 8847360 | tf_op jit(solution)/shard_map/reduce_scatter | solution.py:307
  517.4 161.6 %reduce-scatter.25.cloned.1.call-start = ((), (), s32[]{:S(2)}) async-start(), calls=%async_computation.24 | async-start | bytes 8847360 | tf_op jit(solution)/shard_map/reduce_scatter | solution.py:304
  524.7 221.0 %reduce-scatter.33.cloned.1.call-start = ((), (), s32[]{:S(2)}) async-start(), calls=%async_computation.28 | async-start | bytes 8847360 | tf_op jit(solution)/shard_map/reduce_scatter | solution.py:310
  531.8 280.6 %reduce-scatter.35.cloned.1.call-start = ((), (), s32[]{:S(2)}) async-start(), calls=%async_computation.29 | async-start | bytes 8847360 | tf_op jit(solution)/shard_map/reduce_scatter | solution.py:310
  539.0 340.1 %reduce-scatter.31.cloned.1.call-start = ((), (), s32[]{:S(2)}) async-start(), calls=%async_computation.27 | async-start | bytes 8847360 | tf_op jit(solution)/shard_map/reduce_scatter | solution.py:307
  545.6 400.2 %reduce-scatter.27.cloned.1.call-start = ((), (), s32[]{:S(2)}) async-start(), calls=%async_computation.25 | async-start | bytes 8847360 | tf_op jit(solution)/shard_map/reduce_scatter | solution.py:304
  552.3 464.9 %reduce-scatter.17.cloned.1.call-start = ((), (), s32[]{:S(2)}) async-start(), calls=%async_computation.20 | async-start | bytes 9953280 | tf_op jit(solution)/shard_map/reduce_scatter | solution.py:298
  561.7 527.4 %reduce-scatter.19.cloned.1.call-start = ((), (), s32[]{:S(2)}) async-start(), calls=%async_computation.21 | async-start | bytes 9953280 | tf_op jit(solution)/shard_map/reduce_scatter | solution.py:298
  607.3 604.4 %reduce-scatter.13.cloned.1.call-start = ((), (), s32[]{:S(2)}) async-start(), calls=%async_computation.18 | async-start | bytes 19906560 | tf_op jit(solution)/shard_map/reduce_scatter | solution.py:295
  607.9 6.6 copy-start.104
  623.1 711.1 %reduce-scatter.15.cloned.1.call-start = ((), (), s32[]{:S(2)}) async-start(), calls=%async_computation.19 | async-start | bytes 19906560 | tf_op jit(solution)/shard_map/reduce_scatter | solution.py:295
  625.7 9.1 copy-start.140
  625.7 9.1 copy-start.19
  625.7 9.1 copy-start.130
  653.7 1397.9 %all-reduce.12.cloned.1.call-start = ((), (), s32[]{:S(2)}) async-start(), calls=%async_computation.30 | async-start | bytes 47775744 | tf_op jit(solution)/shard_map/psum | solution.py:229
  1338.8 45.4 %copy-start.90 = (bf16[2,6912]{1,0:T(2,128)(2,1)S(1)}, bf16[2,6912]{1,0:T(2,128)(2,1)}, u32[]{:S(2)}) copy-start(bf16[2,6912]{1,0:T(2,128)(2,1)} %copy-done.89) | copy-start | bytes 82948
  1384.2 9.8 copy-start.92
  1394.0 10.9 copy-start.55
  1394.0 10.9 copy-start.56
  2051.5 7.5 copy-start.68
  2051.5 7.5 copy-start.69
  2051.5 8.7 copy-start.64
  (114 other events, 212.4 us)
Sparse Core Ops, SparseCore 0:
  9.5 103.7 all-gather.6
  114.9 55.8 all-gather.8
  172.4 25.7 all-gather.10
  199.5 50.8 all-gather.12
  251.8 50.8 all-gather.16
  304.1 50.8 all-gather.14
  451.6 34.7 reduce-scatter.20
  510.8 34.7 reduce-scatter.22
  548.2 64.1 reduce-scatter.28
  614.8 64.1 reduce-scatter.24
  681.5 64.1 reduce-scatter.32
  748.2 64.1 reduce-scatter.34
  814.9 64.1 reduce-scatter.30
  881.5 64.1 reduce-scatter.26
  948.2 68.8 reduce-scatter.16
  1020.2 68.8 reduce-scatter.18
  1091.5 120.0 reduce-scatter.12
  1214.1 120.0 reduce-scatter.14
  1340.6 710.8 all-reduce.11
where the time goes:
time: 2090 us; the launch traced here: 2080 us
  waiting for transfers between devices  1610 us (77%)
  matrix products  299 us (14%)
  other arithmetic  61.2 us (3%)
  local copies, waits for them, and re-layouts  45.4 us (2%)
  blocking collectives  44.6 us (2%)
    psum x1, waiting for transfers between devices, sum_data(): lax.psum(grad_parts[0].astype(jnp.bfloat16), 'dp').astype(jnp.float32)  644 us
    reduce_scatter x2, waiting for transfers between devices, shards(): lax.psum_scatter(full_grads[0].astype(jnp.bfloat16), 'fsdp', scatter_dime...  245 us
    reduce_scatter x2, waiting for transfers between devices, shards(): lax.psum_scatter(full_grads[1].astype(jnp.bfloat16), 'fsdp', scatter_dime...  143 us
    reduce_scatter x2, waiting for transfers between devices, shards(): lax.psum_scatter(full_grads[5].astype(jnp.bfloat16), 'fsdp', scatter_dime...  133 us
    all_gather x1, waiting for transfers between devices, shards(): lax.all_gather(w_mod, 'fsdp', axis=0, tiled=True)  97.3 us
    reduce_scatter x2, waiting for transfers between devices, shards(): lax.psum_scatter(full_grads[3].astype(jnp.bfloat16), 'fsdp', scatter_dime...  91.8 us
    reduce_scatter x2, waiting for transfers between devices, shards(): lax.psum_scatter(full_grads[4].astype(jnp.bfloat16), 'fsdp', scatter_dime...  66.8 us
    all_gather x1, waiting for transfers between devices, shards(): lax.all_gather(w_down, 'fsdp', axis=0, tiled=True)  45.2 us
  transfers between devices with their start and end apart: 19, of which 16 were waited for; matrix products, arithmetic and copies ran while one was open for 13% of the time, Pallas kernels for 0%

commit v1 on v0

--- a/solution.py
+++ b/solution.py
@@ -226,7 +226,9 @@
 
 def sum_data(grad_parts):
     return (
-        lax.psum(grad_parts[0].astype(jnp.bfloat16), "dp").astype(jnp.float32),
+        jnp.sum(lax.all_gather(grad_parts[0].astype(jnp.bfloat16), "dp"), axis=0).astype(
+            jnp.float32
+        ),
         lax.psum(grad_parts[1].astype(jnp.bfloat16), "dp").astype(jnp.float32),
         lax.psum(grad_parts[2].astype(jnp.bfloat16), "dp").astype(jnp.float32),
         lax.psum(grad_parts[3].astype(jnp.bfloat16), "dp").astype(jnp.float32),

time: 2090 us -> 3080 us (1.47)
  waiting for transfers between devices: 1610 us -> 2570 us
    all_gather x0 -> x2, waiting for transfers between devices: none -> 1180 us  [sum_data(): lax.all_gather(grad_parts[0].astype(jnp.bfloat16), 'dp')]
    psum x1, waiting for transfers between devices: 644 us -> 419 us  [sum_data(): lax.psum(grad_parts[1].astype(jnp.bfloat16), 'dp').astype(jnp.float32)]
  transfers between devices with their start and end apart: 19 -> 21, of which waited for: 16 -> 18; matrix products, arithmetic and copies ran while one was open for 13% -> 9% of each run, Pallas kernels for 0% -> 0%
where the time goes in v1:
time: 3080 us; the launch traced here: 3070 us
  waiting for transfers between devices  2570 us (83%)
  matrix products  299 us (10%)
  other arithmetic  91.2 us (3%)
  blocking collectives  46.1 us (1%)
  local copies, waits for them, and re-layouts  45.6 us (1%)
    all_gather x2, waiting for transfers between devices, sum_data(): lax.all_gather(grad_parts[0].astype(jnp.bfloat16), 'dp')  1180 us
    psum x1, waiting for transfers between devices, sum_data(): lax.psum(grad_parts[1].astype(jnp.bfloat16), 'dp').astype(jnp.float32)  419 us
    reduce_scatter x2, waiting for transfers between devices, shards(): lax.psum_scatter(full_grads[0].astype(jnp.bfloat16), 'fsdp', scatter_dime...  245 us
    reduce_scatter x2, waiting for transfers between devices, shards(): lax.psum_scatter(full_grads[1].astype(jnp.bfloat16), 'fsdp', scatter_dime...  143 us
    reduce_scatter x2, waiting for transfers between devices, shards(): lax.psum_scatter(full_grads[5].astype(jnp.bfloat16), 'fsdp', scatter_dime...  133 us
    all_gather x1, waiting for transfers between devices, shards(): lax.all_gather(w_mod, 'fsdp', axis=0, tiled=True)  97.4 us
    reduce_scatter x2, waiting for transfers between devices, shards(): lax.psum_scatter(full_grads[3].astype(jnp.bfloat16), 'fsdp', scatter_dime...  91.7 us
    reduce_scatter x2, waiting for transfers between devices, shards(): lax.psum_scatter(full_grads[4].astype(jnp.bfloat16), 'fsdp', scatter_dime...  66.8 us
  transfers between devices with their start and end apart: 21, of which 18 were waited for; matrix products, arithmetic and copies ran while one was open for 9% of the time, Pallas kernels for 0%

profile of v1, /device:TPU:0, one launch (start us, length us, event | category | flops | bytes accessed | tf_op | source)
XLA Modules:
  0.0 3069.2 jit_solution(443894684441338614)
XLA Ops:
  16.0 97.4 %all-gather.11.cloned.1.call-done = bf16[1152,6912]{1,0:T(8,128)(2,1)} async-done(((bf16[288,6912]{1,0:T(8,128)(2,1)}), bf16[1152,6912]{1,0:T(8,128)(2,1)}) %all-gather.11.cloned.1.call-update) | async-done | bytes 15925264 | tf_op jit(solution)/shard_map/all_gather | solution.py:272
  113.4 7.7 convolution_add_fusion.1
  121.1 3.0 fusion.117
  124.1 3.6 copy-done
  128.0 42.8 %all-gather.13.cloned.1.call-done = bf16[1152,3456]{1,0:T(8,128)(2,1)} async-done(((bf16[288,3456]{1,0:T(8,128)(2,1)}), bf16[1152,3456]{1,0:T(8,128)(2,1)}) %all-gather.13.cloned.1.call-update) | async-done | bytes 7962640 | tf_op jit(solution)/shard_map/all_gather | solution.py:273
  170.8 5.8 convolution_add_fusion.3
  187.9 10.2 all-gather.15.cloned.1.call-done
  198.1 4.6 multiply_reduce_fusion.15
  206.6 43.8 %all-gather.17.cloned.1.call-done = bf16[1152,3072]{1,0:T(8,128)(2,1)} async-done(((bf16[288,3072]{1,0:T(8,128)(2,1)}), bf16[1152,3072]{1,0:T(8,128)(2,1)}) %all-gather.17.cloned.1.call-update) | async-done | bytes 7077904 | tf_op jit(solution)/shard_map/all_gather | solution.py:275
  250.4 7.1 fusion.190
  257.5 45.2 %all-gather.21.cloned.1.call-done = bf16[3072,1152]{1,0:T(8,128)(2,1)} async-done(((bf16[768,1152]{1,0:T(8,128)(2,1)}), bf16[3072,1152]{1,0:T(8,128)(2,1)}) %all-gather.21.cloned.1.call-update) | async-done | bytes 7077904 | tf_op jit(solution)/shard_map/all_gather | solution.py:277
  302.7 7.5 fusion.184
  310.1 44.8 %all-gather.19.cloned.1.call-done = bf16[1152,3072]{1,0:T(8,128)(2,1)} async-done(((bf16[288,3072]{1,0:T(8,128)(2,1)}), bf16[1152,3072]{1,0:T(8,128)(2,1)}) %all-gather.19.cloned.1.call-update) | async-done | bytes 7077904 | tf_op jit(solution)/shard_map/all_gather | solution.py:276
  354.9 8.0 multiply_convert_fusion.7
  363.0 7.0 fusion.195
  370.0 4.1 multiply_reduce_fusion.11
  386.3 3.5 fusion.95
  392.6 9.8 fusion.44
  402.4 10.1 fusion.47
  418.1 8.1 convolution_add_fusion
  429.3 10.9 fusion.78
  440.3 3.4 fusion.55
  443.7 6.5 convolution_add_fusion.2
  467.2 4.0 fusion.193
  471.2 4.0 fusion.192
  475.1 10.0 multiply_convert_fusion.2
  485.2 6.4 fusion.197
  491.7 6.2 multiply_reduce_fusion.8
  510.8 6.6 convolution_convert_fusion.7
  517.9 6.9 convolution_convert_fusion.9
  524.9 7.0 convolution_convert_fusion.5
  531.9 7.0 convolution_convert_fusion.4
  539.0 6.5 convolution_convert_fusion.6
  545.6 6.6 convolution_convert_fusion.8
  552.2 9.3 convolution_convert_fusion.3
  561.8 4.0 convolution_convert_fusion.12
  567.9 4.4 fusion.198
  572.3 9.7 fusion.38
  582.1 9.9 fusion.41
  601.3 6.0 convolution_convert_fusion.2
  608.0 6.0 fusion.188
  614.6 8.7 convolution_convert_fusion.1
  625.9 9.1 fusion.80
  642.3 3.0 fusion.189
  645.9 7.9 convolution_convert_fusion
  653.9 25.1 reduce-scatter.25.cloned.1.call-done
  679.0 66.8 %reduce-scatter.33.cloned.1.call-done = bf16[768,1152]{1,0:T(8,128)(2,1)} async-done(((bf16[3072,1152]{1,0:T(8,128)(2,1)}), bf16[768,1152]{1,0:T(8,128)(2,1)}) %reduce-scatter.33.cloned.1.call-update) | async-done | bytes 1769488 | tf_op jit(solution)/shard_map/reduce_scatter | solution.py:312
  745.8 66.6 %reduce-scatter.35.cloned.1.call-done = bf16[768,1152]{1,0:T(8,128)(2,1)} async-done(((bf16[3072,1152]{1,0:T(8,128)(2,1)}), bf16[768,1152]{1,0:T(8,128)(2,1)}) %reduce-scatter.35.cloned.1.call-update) | async-done | bytes 1769488 | tf_op jit(solution)/shard_map/reduce_scatter | solution.py:312
  812.4 66.8 %reduce-scatter.31.cloned.1.call-done = bf16[288,3072]{1,0:T(8,128)(2,1)} async-done(((bf16[1152,3072]{1,0:T(8,128)(2,1)}), bf16[288,3072]{1,0:T(8,128)(2,1)}) %reduce-scatter.31.cloned.1.call-update) | async-done | bytes 1769488 | tf_op jit(solution)/shard_map/reduce_scatter | solution.py:309
  879.2 66.6 %reduce-scatter.27.cloned.1.call-done = bf16[288,3072]{1,0:T(8,128)(2,1)} async-done(((bf16[1152,3072]{1,0:T(8,128)(2,1)}), bf16[288,3072]{1,0:T(8,128)(2,1)}) %reduce-scatter.27.cloned.1.call-update) | async-done | bytes 1769488 | tf_op jit(solution)/shard_map/reduce_scatter | solution.py:306
  945.8 71.3 %reduce-scatter.17.cloned.1.call-done = bf16[288,3456]{1,0:T(8,128)(2,1)} async-done(((bf16[1152,3456]{1,0:T(8,128)(2,1)}), bf16[288,3456]{1,0:T(8,128)(2,1)}) %reduce-scatter.17.cloned.1.call-update) | async-done | bytes 1990672 | tf_op jit(solution)/shard_map/reduce_scatter | solution.py:300
  1017.1 71.9 %reduce-scatter.19.cloned.1.call-done = bf16[288,3456]{1,0:T(8,128)(2,1)} async-done(((bf16[1152,3456]{1,0:T(8,128)(2,1)}), bf16[288,3456]{1,0:T(8,128)(2,1)}) %reduce-scatter.19.cloned.1.call-update) | async-done | bytes 1990672 | tf_op jit(solution)/shard_map/reduce_scatter | solution.py:300
  1089.1 122.5 %reduce-scatter.13.cloned.1.call-done = bf16[288,6912]{1,0:T(8,128)(2,1)} async-done(((bf16[1152,6912]{1,0:T(8,128)(2,1)}), bf16[288,6912]{1,0:T(8,128)(2,1)}) %reduce-scatter.13.cloned.1.call-update) | async-done | bytes 3981328 | tf_op jit(solution)/shard_map/reduce_scatter | solution.py:297
  1211.6 122.5 %reduce-scatter.15.cloned.1.call-done = bf16[288,6912]{1,0:T(8,128)(2,1)} async-done(((bf16[1152,6912]{1,0:T(8,128)(2,1)}), bf16[288,6912]{1,0:T(8,128)(2,1)}) %reduce-scatter.15.cloned.1.call-update) | async-done | bytes 3981328 | tf_op jit(solution)/shard_map/reduce_scatter | solution.py:297
  1339.7 46.1 %all-reduce.8 = (f32[6912]{0:T(1024)}, f32[3456]{0:T(1024)}, f32[72]{0:T(128)}, f32[72]{0:T(128)}, f32[1152]{0:T(1024)}) all-reduce(f32[6912]{0:T(1024)S(1)} %add.438, f32[3456]{0:T(1024)S(1)} %add.440, f32[72]{0:T(128)S(1)} %copy-done.142, f32[72]{0:T(128)S(1)} %add.442, ...), channel_id=1, replica_groups=mesh['dp'=8,'fsdp'=4] {'dp','fsdp'}, use_global_device_ids=true, to_apply=%region_34.35 | all-reduce | flops 11664 | bytes 93312 | tf_op jit(solution)/shard_map/psum | solution.py:319
  1385.8 9.9 fusion.28
  1395.7 10.2 fusion.29
  1409.3 418.7 %all-reduce.12.cloned.1.call-done = (bf16[288,3456]{1,0:T(8,128)(2,1)}, bf16[288,3456]{1,0:T(8,128)(2,1)}, bf16[288,1152]{1,0:T(8,128)(2,1)}, bf16[288,1152]{1,0...) async-done(((bf16[288,3456]{1,0:T(8,128)(2,1)}, ...) | async-done | bytes 15925264 | tf_op jit(solution)/shard_map/psum | solution.py:232
  1830.6 3.9 convert_add_fusion.2
  1844.1 589.9 %all-gather.23.cloned.1.call-done = bf16[2304,6912]{1,0:T(8,128)(2,1)} async-done(((bf16[288,6912]{1,0:T(8,128)(2,1)}), bf16[2304,6912]{1,0:T(8,128)(2,1)}) %all-gather.23.cloned.1.call-update) | async-done | bytes 31850512 | tf_op jit(solution)/shard_map/all_gather | solution.py:229
  2434.0 14.5 reduce_sum.366
  2448.5 592.7 %all-gather.25.cloned.1.call-done = bf16[2304,6912]{1,0:T(8,128)(2,1)} async-done(((bf16[288,6912]{1,0:T(8,128)(2,1)}), bf16[2304,6912]{1,0:T(8,128)(2,1)}) %all-gather.25.cloned.1.call-update) | async-done | bytes 31850512 | tf_op jit(solution)/shard_map/all_gather | solution.py:229
  3041.2 13.6 reduce_sum.370
  3054.8 7.4 convert_add_fusion
  (473 shorter events, 122.2 us)
Async XLA Ops:
  7.2 106.2 %all-gather.11.cloned.1.call-start = ((), (), s32[]{:S(2)}) async-start(), calls=%async_computation.12 | async-start | bytes 19906560 | tf_op jit(solution)/shard_map/all_gather | solution.py:272
  7.9 162.9 %all-gather.13.cloned.1.call-start = ((), (), s32[]{:S(2)}) async-start(), calls=%async_computation.13 | async-start | bytes 9953280 | tf_op jit(solution)/shard_map/all_gather | solution.py:273
  8.7 189.5 %all-gather.15.cloned.1.call-start = ((), (), s32[]{:S(2)}) async-start(), calls=%async_computation.14 | async-start | bytes 3317760 | tf_op jit(solution)/shard_map/all_gather | solution.py:274
  9.4 241.0 %all-gather.17.cloned.1.call-start = ((), (), s32[]{:S(2)}) async-start(), calls=%async_computation.15 | async-start | bytes 8847360 | tf_op jit(solution)/shard_map/all_gather | solution.py:275
  10.0 292.7 %all-gather.21.cloned.1.call-start = ((), (), s32[]{:S(2)}) async-start(), calls=%async_computation.17 | async-start | bytes 8847360 | tf_op jit(solution)/shard_map/all_gather | solution.py:277
  10.6 102.8 %copy-start.101 = (bf16[2,1,2,1152]{3,2,1,0:T(2,128)(2,1)S(1)}, bf16[2,1,2,1152]{3,2,1,0:T(2,128)(2,1)}, u32[]{:S(2)}) copy-start(bf16[2,1,2,1152]{3,2,1,0:T(2,128)(2,1)} %param.16) | copy-start | bytes 27652
  10.6 102.8 %copy-start.104 = (f32[6912]{0:T(1024)S(1)}, f32[6912]{0:T(1024)}, u32[]{:S(2)}) copy-start(f32[6912]{0:T(1024)} %param.19) | copy-start | bytes 82948
  10.6 344.3 %all-gather.19.cloned.1.call-start = ((), (), s32[]{:S(2)}) async-start(), calls=%async_computation.16 | async-start | bytes 8847360 | tf_op jit(solution)/shard_map/all_gather | solution.py:276
  11.2 642.7 %reduce-scatter.21.cloned.1.call-start = ((), (), s32[]{:S(2)}) async-start(), calls=%async_computation.22 | async-start | bytes 3317760 | tf_op jit(solution)/shard_map/reduce_scatter | solution.py:303
  11.7 109.3 %copy-start.111 = (s32[256]{0:T(256)}, s32[256]{0:T(256)S(1)}, u32[]{:S(2)}) copy-start(s32[256]{0:T(256)S(1)} %compare_convert_fusion.1) | copy-start | bytes 3076
  14.5 109.5 %copy-start.132 = (f32[256]{0:T(256)}, f32[256]{0:T(256)S(1)}, u32[]{:S(2)}) copy-start(f32[256]{0:T(256)S(1)} %fusion.126) | copy-start | bytes 3076
  127.7 43.1 %copy-start.144 = (f32[3456]{0:T(1024)S(1)}, f32[3456]{0:T(1024)}, u32[]{:S(2)}) copy-start(f32[3456]{0:T(1024)} %param.21) | copy-start | bytes 41476
  128.0 48.6 %copy-start.49 = (bf16[256,1152]{1,0:T(8,128)(2,1)}, bf16[256,1152]{1,0:T(8,128)(2,1)S(1)}, u32[]{:S(2)}) copy-start(bf16[256,1152]{1,0:T(8,128)(2,1)S(1)} %fusion.54) | copy-start | bytes 1769476
  202.7 173.9 %copy-start.2 = (f32[256,1152]{1,0:T(8,128)}, f32[256,1152]{1,0:T(8,128)S(1)}, u32[]{:S(2)}) copy-start(f32[256,1152]{1,0:T(8,128)S(1)} %get-tuple-element.53) | copy-start | bytes 3538948
  362.9 7.0 copy-start.66
  363.0 7.0 copy-start.67
  363.0 11.2 copy-start.45
  363.0 7.0 copy-start.143
  363.0 11.2 slice-start.4
  370.0 4.2 copy-start.135
  370.0 4.2 slice-start.5
  370.0 6.5 slice-start
  389.8 39.4 %copy-start.29 = (f32[16,72,256]{2,1,0:T(8,128)}, f32[16,72,256]{2,1,0:T(8,128)S(1)}, u32[]{:S(2)}) copy-start(f32[16,72,256]{2,1,0:T(8,128)S(1)} %fusion.95) | copy-start | bytes 3538948
  416.0 13.3 copy-start.11
  418.1 11.2 copy-start.13
  418.1 8.1 copy-start.109
  429.2 11.0 copy-start.1
  429.3 11.0 copy-start.131
  429.3 11.0 copy-start.133
  443.6 6.5 copy-start.47
  451.4 202.5 %reduce-scatter.23.cloned.1.call-start = ((), (), s32[]{:S(2)}) async-start(), calls=%async_computation.23 | async-start | bytes 3317760 | tf_op jit(solution)/shard_map/reduce_scatter | solution.py:303
  457.8 5.6 slice-start.2
  458.8 4.6 slice-start.3
  462.3 4.9 slice-start.10
  466.8 38.4 %copy-start.126 = (f32[256]{0:T(256)}, f32[256]{0:T(256)S(1)}, u32[]{:S(2)}) copy-start(f32[256]{0:T(256)S(1)} %fusion.129) | copy-start | bytes 3076
  466.8 4.3 slice-start.8
  485.2 6.4 copy-start.68
  485.2 17.8 copy-start.46
  485.2 17.8 slice-start.6
  491.6 6.2 copy-start.22
  491.6 6.2 copy-start.37
  491.7 11.3 slice-start.7
  497.8 7.4 copy-start.24
  510.7 143.2 %reduce-scatter.29.cloned.1.call-start = ((), (), s32[]{:S(2)}) async-start(), calls=%async_computation.26 | async-start | bytes 8847360 | tf_op jit(solution)/shard_map/reduce_scatter | solution.py:309
  517.4 161.6 %reduce-scatter.25.cloned.1.call-start = ((), (), s32[]{:S(2)}) async-start(), calls=%async_computation.24 | async-start | bytes 8847360 | tf_op jit(solution)/shard_map/reduce_scatter | solution.py:306
  524.8 221.0 %reduce-scatter.33.cloned.1.call-start = ((), (), s32[]{:S(2)}) async-start(), calls=%async_computation.28 | async-start | bytes 8847360 | tf_op jit(solution)/shard_map/reduce_scatter | solution.py:312
  531.9 280.5 %reduce-scatter.35.cloned.1.call-start = ((), (), s32[]{:S(2)}) async-start(), calls=%async_computation.29 | async-start | bytes 8847360 | tf_op jit(solution)/shard_map/reduce_scatter | solution.py:312
  539.0 340.2 %reduce-scatter.31.cloned.1.call-start = ((), (), s32[]{:S(2)}) async-start(), calls=%async_computation.27 | async-start | bytes 8847360 | tf_op jit(solution)/shard_map/reduce_scatter | solution.py:309
  545.5 400.2 %reduce-scatter.27.cloned.1.call-start = ((), (), s32[]{:S(2)}) async-start(), calls=%async_computation.25 | async-start | bytes 8847360 | tf_op jit(solution)/shard_map/reduce_scatter | solution.py:306
  552.2 465.0 %reduce-scatter.17.cloned.1.call-start = ((), (), s32[]{:S(2)}) async-start(), calls=%async_computation.20 | async-start | bytes 9953280 | tf_op jit(solution)/shard_map/reduce_scatter | solution.py:300
  561.6 527.5 %reduce-scatter.19.cloned.1.call-start = ((), (), s32[]{:S(2)}) async-start(), calls=%async_computation.21 | async-start | bytes 9953280 | tf_op jit(solution)/shard_map/reduce_scatter | solution.py:300
  607.3 604.2 %reduce-scatter.13.cloned.1.call-start = ((), (), s32[]{:S(2)}) async-start(), calls=%async_computation.18 | async-start | bytes 19906560 | tf_op jit(solution)/shard_map/reduce_scatter | solution.py:297
  608.0 6.6 copy-start.103
  623.3 710.8 %reduce-scatter.15.cloned.1.call-start = ((), (), s32[]{:S(2)}) async-start(), calls=%async_computation.19 | async-start | bytes 19906560 | tf_op jit(solution)/shard_map/reduce_scatter | solution.py:297
  625.9 9.1 copy-start.139
  625.9 9.1 copy-start.20
  625.9 9.1 copy-start.129
  653.8 1174.2 %all-reduce.12.cloned.1.call-start = ((), (), s32[]{:S(2)}) async-start(), calls=%async_computation.32 | async-start | bytes 31850496 | tf_op jit(solution)/shard_map/psum | solution.py:232
  1089.1 1344.9 %all-gather.23.cloned.1.call-start = ((), (), s32[]{:S(2)}) async-start(), calls=%async_computation.30 | async-start | bytes 35831808 | tf_op jit(solution)/shard_map/all_gather | solution.py:229
  1211.6 1829.6 %all-gather.25.cloned.1.call-start = ((), (), s32[]{:S(2)}) async-start(), calls=%async_computation.31 | async-start | bytes 35831808 | tf_op jit(solution)/shard_map/all_gather | solution.py:229
  1338.9 46.9 %copy-start.89 = (bf16[2,6912]{1,0:T(2,128)(2,1)S(1)}, bf16[2,6912]{1,0:T(2,128)(2,1)}, u32[]{:S(2)}) copy-start(bf16[2,6912]{1,0:T(2,128)(2,1)} %copy-done.88) | copy-start | bytes 82948
  1385.8 9.9 copy-start.91
  1395.7 10.9 copy-start.57
  1395.7 10.9 copy-start.58
  (115 other events, 215.9 us)
Sparse Core Ops, SparseCore 0:
  9.5 103.7 all-gather.10
  114.9 55.8 all-gather.12
  172.4 25.7 all-gather.14
  199.5 50.8 all-gather.16
  251.8 50.8 all-gather.20
  304.1 50.8 all-gather.18
  451.5 34.7 reduce-scatter.20
  510.9 34.7 reduce-scatter.22
  548.2 64.1 reduce-scatter.28
  614.8 64.1 reduce-scatter.24
  681.6 64.1 reduce-scatter.32
  748.2 64.1 reduce-scatter.34
  814.9 64.1 reduce-scatter.30
  881.6 64.1 reduce-scatter.26
  948.2 68.8 reduce-scatter.16
  1020.2 68.8 reduce-scatter.18
  1091.5 120.0 reduce-scatter.12
  1214.0 120.0 reduce-scatter.14
  1340.5 487.4 all-reduce.11
  1829.4 604.5 all-gather.22
  2435.5 605.6 all-gather.24
